TPU v7x, 32 devices: a whole 2x2x4 slice. The times are simulated.
32 devices in a mesh: prec: 16 (over z, x, core), run: 2 (over y).
Axes of the slice: x: 2, y: 2, z: 4, core: 2. Of those that a mesh axis runs over, the one named last changes fastest.
Arguments:
- intensity: bfloat16 [1024, 32768], P('run', 'prec'), may hold values from -6 to 6
- observed: int32 [1024, 4096], P('run', 'prec'), may hold values from 0 to 255, as said below
- run_factors: bfloat16 [1024, 64], P('run'), as said below
- prec_factors: bfloat16 [32768, 64], P('prec'), as said below
Outputs:
- completed: bfloat16 [1024, 32768], P('run', 'prec')
Inputs may be any that keep to these rules, and one draw needn't show every extreme that they name: `observed`: each word packs eight observation flags in its low 8 bits: bit b of word j is the flag of precursor 8 j + b. `run_factors`: rows of the starting factors have scales that vary along the rows. `prec_factors`: rows of the starting factors have scales that vary along the rows.
All inputs are finite; a program needn't handle non-finite values.
Results may differ from a plain program's by a relative error of at most 0.005.
Values may be sent and summed in bfloat16 or wider, within the bound.
A program may use at most 64 MiB of HBM per device.

v0:
```python
import jax
import jax.numpy as jnp
from jax import lax
from jax.sharding import PartitionSpec as P

ITERS = 4
ridge_value = 16.0


def unpack_mask(words):
    shifts = jnp.arange(8, dtype=jnp.int32)
    bits = jnp.right_shift(words[:, :, None], shifts) & 1
    return bits.reshape(words.shape[0], -1).astype(jnp.float32)


def ridge_solve(matrix, gram):
    size = gram.shape[0]
    factor = jnp.linalg.cholesky(gram + ridge_value * jnp.eye(size, dtype=jnp.float32))
    return jax.scipy.linalg.cho_solve((factor, True), matrix.T).T


def inner_gram(factors):
    return lax.dot_general(
        factors, factors, (((0,), (0,)), ((), ())), preferred_element_type=jnp.float32
    )


def masked_resid(intensity, maskf, u_now, v_now):
    fit = jnp.dot(u_now, v_now.T, preferred_element_type=jnp.float32)
    return (maskf * (intensity.astype(jnp.float32) - fit)).astype(jnp.bfloat16)


def local(intensity, observed, run_factors, prec_factors):
    maskf = unpack_mask(observed)
    u_now = run_factors
    v_now = prec_factors
    for step in range(ITERS):
        resid = masked_resid(intensity, maskf, u_now, v_now)
        proj_part = jnp.dot(resid, v_now, preferred_element_type=jnp.float32)
        gram_part = inner_gram(v_now)
        gram_v = lax.psum(gram_part, "prec")
        share = lax.psum_scatter(proj_part, "prec", scatter_dimension=0, tiled=True)
        count = share.shape[0]
        first = lax.axis_index("prec") * count
        mine = lax.dynamic_slice_in_dim(u_now, first, count, 0)
        total = jnp.dot(mine.astype(jnp.float32), gram_v, precision=lax.Precision.HIGHEST) + share
        fresh = ridge_solve(total, gram_v).astype(jnp.bfloat16)
        u_now = lax.all_gather(fresh, "prec", axis=0, tiled=True)
        resid = masked_resid(intensity, maskf, u_now, v_now)
        proj_part = lax.dot_general(
            resid, u_now, (((0,), (0,)), ((), ())), preferred_element_type=jnp.float32
        )
        gram_part = inner_gram(u_now)
        proj_v, gram_u = (
            lax.psum(proj_part.astype(jnp.bfloat16), "run").astype(jnp.float32),
            lax.psum(gram_part.astype(jnp.bfloat16), "run").astype(jnp.float32),
        )
        total = jnp.dot(v_now.astype(jnp.float32), gram_u, precision=lax.Precision.HIGHEST) + proj_v
        v_now = ridge_solve(total, gram_u).astype(jnp.bfloat16)
    fit = jnp.dot(u_now, v_now.T, preferred_element_type=jnp.float32)
    return (maskf * intensity.astype(jnp.float32) + (1.0 - maskf) * fit).astype(jnp.bfloat16)


def solution(mesh):
    return jax.shard_map(
        local,
        mesh=mesh,
        in_specs=(P("run", "prec"), P("run", "prec"), P("run", None), P("prec", None)),
        out_specs=P("run", "prec"),
        check_vma=False,
    )
```

profile of v0, /device:TPU:0, one launch (start us, length us, event | category | flops | bytes accessed | tf_op | source)
XLA Modules:
  0.0 746.3 jit_solution(6776300041927255322)
XLA Ops:
  10.3 5.5 copy.22
  20.7 63.0 %psum.84 = f32[64,64]{0,1:T(8,128)S(1)} all-reduce(f32[64,64]{0,1:T(8,128)S(1)} %fusion.103), channel_id=1, replica_groups=mesh['prec'=16,'run'=2] {'prec'}, use_global_device_ids=true, to_apply=%region_0.0 | all-reduce | flops 4096 | bytes 32768 | tf_op jit(solution)/shard_map/psum | solution.py:41
  83.7 5.8 cholesky.134
  90.9 4.9 custom-call.18
  97.3 17.5 %all_gather.12 = bf16[512,64]{1,0:T(8,128)(2,1)S(1)} all-gather(bf16[32,64]{1,0:T(8,128)(2,1)S(1)} %fusion.31), channel_id=1, replica_groups=mesh['prec'=16,'run'=2] {'prec'}, dimensions={0}, use_global_device_ids=true | all-gather | bytes 69632 | tf_op jit(solution)/shard_map/all_gather | solution.py:48
  119.3 8.2 %psum.85 = bf16[64,64]{0,1:T(8,128)(2,1)S(1)} all-reduce(bf16[64,64]{0,1:T(8,128)(2,1)S(1)} %convolution_convert_fusion.11), channel_id=1, replica_groups=mesh['prec'=16,'run'=2] {'run'}, use_global_device_ids=true, to_apply=%region_4.7 | all-reduce | flops 4096 | bytes 16384 | tf_op jit(solution)/shard_map/psum | solution.py:56
  127.6 5.9 cholesky.145
  139.7 15.1 %all-reduce.5.cloned.1.call-done = bf16[2048,64]{0,1:T(8,128)(2,1)} async-done(((bf16[2048,64]{0,1:T(8,128)(2,1)}), bf16[2048,64]{0,1:T(8,128)(2,1)}) %all-reduce.5.cloned.1.call-update) | async-done | bytes 262160 | tf_op jit(solution)/shard_map/psum | solution.py:55
  161.7 61.2 %psum.87 = f32[64,64]{0,1:T(8,128)S(1)} all-reduce(f32[64,64]{0,1:T(8,128)S(1)} %fusion.104), channel_id=1, replica_groups=mesh['prec'=16,'run'=2] {'prec'}, use_global_device_ids=true, to_apply=%region_6.0 | all-reduce | flops 4096 | bytes 32768 | tf_op jit(solution)/shard_map/psum | solution.py:41
  223.0 5.8 cholesky.156
  230.3 4.9 custom-call.20
  235.2 46.6 %reduce-scatter.7.cloned.1.call-done = f32[32,64]{1,0:T(8,128)} async-done(((f32[512,64]{1,0:T(8,128)}), f32[32,64]{1,0:T(8,128)}) %reduce-scatter.7.cloned.1.call-update) | async-done | bytes 8208 | tf_op jit(solution)/shard_map/reduce_scatter | solution.py:42
  283.2 19.8 %all_gather.13 = bf16[512,64]{1,0:T(8,128)(2,1)S(1)} all-gather(bf16[32,64]{1,0:T(8,128)(2,1)S(1)} %fusion.32), channel_id=1, replica_groups=mesh['prec'=16,'run'=2] {'prec'}, dimensions={0}, use_global_device_ids=true | all-gather | bytes 69632 | tf_op jit(solution)/shard_map/all_gather | solution.py:48
  307.7 8.1 %psum.88 = bf16[64,64]{0,1:T(8,128)(2,1)S(1)} all-reduce(bf16[64,64]{0,1:T(8,128)(2,1)S(1)} %convolution_convert_fusion.10), channel_id=1, replica_groups=mesh['prec'=16,'run'=2] {'run'}, use_global_device_ids=true, to_apply=%region_8.0 | all-reduce | flops 4096 | bytes 16384 | tf_op jit(solution)/shard_map/psum | solution.py:56
  316.0 5.8 cholesky.167
  323.1 4.9 custom-call.21
  328.0 19.0 %all-reduce.7.cloned.1.call-done = bf16[2048,64]{1,0:T(8,128)(2,1)} async-done(((bf16[2048,64]{1,0:T(8,128)(2,1)}), bf16[2048,64]{1,0:T(8,128)(2,1)}) %all-reduce.7.cloned.1.call-update) | async-done | bytes 262160 | tf_op jit(solution)/shard_map/psum | solution.py:55
  354.8 61.0 %psum.90 = f32[64,64]{0,1:T(8,128)S(1)} all-reduce(f32[64,64]{0,1:T(8,128)S(1)} %fusion.105), channel_id=1, replica_groups=mesh['prec'=16,'run'=2] {'prec'}, use_global_device_ids=true, to_apply=%region_10.0 | all-reduce | flops 4096 | bytes 32768 | tf_op jit(solution)/shard_map/psum | solution.py:41
  415.9 5.8 cholesky.178
  423.2 4.9 custom-call.22
  428.1 46.6 %reduce-scatter.9.cloned.1.call-done = f32[32,64]{1,0:T(8,128)} async-done(((f32[512,64]{1,0:T(8,128)}), f32[32,64]{1,0:T(8,128)}) %reduce-scatter.9.cloned.1.call-update) | async-done | bytes 8208 | tf_op jit(solution)/shard_map/reduce_scatter | solution.py:42
  476.1 19.9 %all_gather.14 = bf16[512,64]{1,0:T(8,128)(2,1)S(1)} all-gather(bf16[32,64]{1,0:T(8,128)(2,1)S(1)} %fusion.33), channel_id=1, replica_groups=mesh['prec'=16,'run'=2] {'prec'}, dimensions={0}, use_global_device_ids=true | all-gather | bytes 69632 | tf_op jit(solution)/shard_map/all_gather | solution.py:48
  500.8 8.1 %psum.91 = bf16[64,64]{0,1:T(8,128)(2,1)S(1)} all-reduce(bf16[64,64]{0,1:T(8,128)(2,1)S(1)} %convolution_convert_fusion.9), channel_id=1, replica_groups=mesh['prec'=16,'run'=2] {'run'}, use_global_device_ids=true, to_apply=%region_12.0 | all-reduce | flops 4096 | bytes 16384 | tf_op jit(solution)/shard_map/psum | solution.py:56
  509.0 5.8 cholesky.189
  521.0 19.0 %all-reduce.9.cloned.1.call-done = bf16[2048,64]{1,0:T(8,128)(2,1)} async-done(((bf16[2048,64]{1,0:T(8,128)(2,1)}), bf16[2048,64]{1,0:T(8,128)(2,1)}) %all-reduce.9.cloned.1.call-update) | async-done | bytes 262160 | tf_op jit(solution)/shard_map/psum | solution.py:55
  547.9 61.0 %psum.93 = f32[64,64]{0,1:T(8,128)S(1)} all-reduce(f32[64,64]{0,1:T(8,128)S(1)} %fusion.106), channel_id=1, replica_groups=mesh['prec'=16,'run'=2] {'prec'}, use_global_device_ids=true, to_apply=%region_14.0 | all-reduce | flops 4096 | bytes 32768 | tf_op jit(solution)/shard_map/psum | solution.py:41
  609.0 5.8 cholesky.200
  621.1 46.6 %reduce-scatter.11.cloned.1.call-done = f32[32,64]{1,0:T(8,128)} async-done(((f32[512,64]{1,0:T(8,128)}), f32[32,64]{1,0:T(8,128)}) %reduce-scatter.11.cloned.1.call-update) | async-done | bytes 8208 | tf_op jit(solution)/shard_map/reduce_scatter | solution.py:42
  669.1 19.8 %all_gather.15 = bf16[512,64]{1,0:T(8,128)(2,1)S(1)} all-gather(bf16[32,64]{1,0:T(8,128)(2,1)S(1)} %fusion.34), channel_id=1, replica_groups=mesh['prec'=16,'run'=2] {'prec'}, dimensions={0}, use_global_device_ids=true | all-gather | bytes 69632 | tf_op jit(solution)/shard_map/all_gather | solution.py:48
  693.7 8.3 %psum.94 = bf16[64,64]{0,1:T(8,128)(2,1)S(1)} all-reduce(bf16[64,64]{0,1:T(8,128)(2,1)S(1)} %convolution_convert_fusion.8), channel_id=1, replica_groups=mesh['prec'=16,'run'=2] {'run'}, use_global_device_ids=true, to_apply=%region_16.20 | all-reduce | flops 4096 | bytes 16384 | tf_op jit(solution)/shard_map/psum | solution.py:56
  702.1 5.8 cholesky.211
  714.1 19.1 %all-reduce.11.cloned.1.call-done = bf16[2048,64]{1,0:T(8,128)(2,1)} async-done(((bf16[2048,64]{1,0:T(8,128)(2,1)}), bf16[2048,64]{1,0:T(8,128)(2,1)}) %all-reduce.11.cloned.1.call-update) | async-done | bytes 262160 | tf_op jit(solution)/shard_map/psum | solution.py:55
  (122 shorter events, 92.2 us)
Async XLA Ops:
  6.5 9.4 %copy-start = (bf16[2048,64]{0,1:T(8,128)(2,1)S(1)}, bf16[2048,64]{0,1:T(8,128)(2,1)}, u32[]{:S(2)}) copy-start(bf16[2048,64]{0,1:T(8,128)(2,1)} %param.12) | copy-start | bytes 786436
  6.5 89.3 %reduce-scatter.5.cloned.1.call-start = ((), (), s32[]{:S(2)}) async-start(), calls=%async_computation.4 | async-start | bytes 278528 | tf_op jit(solution)/shard_map/reduce_scatter | solution.py:42
  10.3 5.7 copy-start.2
  10.3 5.7 copy-start.3
  20.4 134.4 %all-reduce.5.cloned.1.call-start = ((), (), s32[]{:S(2)}) async-start(), calls=%async_computation.5 | async-start | bytes 524288 | tf_op jit(solution)/shard_map/psum | solution.py:55
  133.5 148.3 %reduce-scatter.7.cloned.1.call-start = ((), (), s32[]{:S(2)}) async-start(), calls=%async_computation.6 | async-start | bytes 278528 | tf_op jit(solution)/shard_map/reduce_scatter | solution.py:42
  229.6 117.4 %all-reduce.7.cloned.1.call-start = ((), (), s32[]{:S(2)}) async-start(), calls=%async_computation.7 | async-start | bytes 1048576 | tf_op jit(solution)/shard_map/psum | solution.py:55
  321.9 152.8 %reduce-scatter.9.cloned.1.call-start = ((), (), s32[]{:S(2)}) async-start(), calls=%async_computation.8 | async-start | bytes 278528 | tf_op jit(solution)/shard_map/reduce_scatter | solution.py:42
  422.5 117.6 %all-reduce.9.cloned.1.call-start = ((), (), s32[]{:S(2)}) async-start(), calls=%async_computation.9 | async-start | bytes 1048576 | tf_op jit(solution)/shard_map/psum | solution.py:55
  514.9 152.8 %reduce-scatter.11.cloned.1.call-start = ((), (), s32[]{:S(2)}) async-start(), calls=%async_computation.10 | async-start | bytes 278528 | tf_op jit(solution)/shard_map/reduce_scatter | solution.py:42
  615.6 117.6 %all-reduce.11.cloned.1.call-start = ((), (), s32[]{:S(2)}) async-start(), calls=%async_computation.11 | async-start | bytes 1048576 | tf_op jit(solution)/shard_map/psum | solution.py:55
  733.2 3.4 copy-start.1
Sparse Core Ops, SparseCore 0:
  20.5 58.5 reduce-scatter.4
  133.6 21.0 all-reduce.4
  229.7 52.0 reduce-scatter.6
  322.0 24.9 all-reduce.6
  422.6 52.0 reduce-scatter.8
  515.0 24.9 all-reduce.8
  615.7 52.0 reduce-scatter.10
  708.2 24.9 all-reduce.10
where the time goes:
time: 755 us; the launch traced here: 746 us
  blocking collectives  356 us (47%)
  waiting for transfers between devices  212 us (28%)
  other arithmetic  96.2 us (13%)
  matrix products  57.4 us (8%)
  between operations  14.2 us (2%)
  local copies, waits for them, and re-layouts  10 us (1%)
    psum x4, blocking collectives, local(): gram_v = lax.psum(gram_part, 'prec')  246 us
    reduce_scatter x4, waiting for transfers between devices, local(): share = lax.psum_scatter(proj_part, 'prec', scatter_dimension=0, tiled=True)  140 us
    all_gather x4, blocking collectives, local(): u_now = lax.all_gather(fresh, 'prec', axis=0, tiled=True)  77 us
    psum x4, waiting for transfers between devices, local(): lax.psum(proj_part.astype(jnp.bfloat16), 'run').astype(jnp.float32)  72.2 us
    another operation x24, other arithmetic, ridge_solve(): jnp.linalg.cholesky(gram + ridge_value * jnp.eye(size, dtype=jnp.float32))  52.2 us
    another operation x16, other arithmetic, ridge_solve(): return jax.scipy.linalg.cho_solve((factor, True), matrix.T).T  43.9 us
    psum x4, blocking collectives, local(): lax.psum(gram_part.astype(jnp.bfloat16), 'run').astype(jnp.float32)  32.7 us
    dot_general x4, matrix products, local(): lax.dot_general(resid, u_now, (((0,), (0,)), ((), ())), preferred_element...  18.1 us
  transfers between devices with their start and end apart: 8, of which 7 were waited for; matrix products, arithmetic and copies ran while one was open for 7% of the time, Pallas kernels for 0%

commit v1 on v0

--- a/solution.py
+++ b/solution.py
@@ -38,7 +38,7 @@
         resid = masked_resid(intensity, maskf, u_now, v_now)
         proj_part = jnp.dot(resid, v_now, preferred_element_type=jnp.float32)
         gram_part = inner_gram(v_now)
-        gram_v = lax.psum(gram_part, "prec")
+        gram_v = jnp.sum(lax.all_gather(gram_part, "prec"), axis=0)
         share = lax.psum_scatter(proj_part, "prec", scatter_dimension=0, tiled=True)
         count = share.shape[0]
         first = lax.axis_index("prec") * count

time: 755 us -> 607 us (0.80)
  blocking collectives: 356 us -> 206 us
    psum x4 -> x0, blocking collectives: 246 us -> none  [local(): gram_v = lax.psum(gram_part, 'prec')]
    all_gather x0 -> x4, blocking collectives: none -> 93.7 us  [local(): gram_v = jnp.sum(lax.all_gather(gram_part, 'prec'), axis=0)]
    reduce_scatter x4, waiting for transfers between devices: 140 us -> 161 us  [local(): share = lax.psum_scatter(proj_part, 'prec', scatter_dimension=0, tiled=True)]
    psum x4, waiting for transfers between devices: 72.2 us -> 54.4 us  [local(): lax.psum(proj_part.astype(jnp.bfloat16), 'run').astype(jnp.float32)]
  transfers between devices with their start and end apart: 8 -> 8, of which waited for: 7 -> 8; matrix products, arithmetic and copies ran while one was open for 7% -> 9% of each run, Pallas kernels for 0% -> 0%
where the time goes in v1:
time: 607 us; the launch traced here: 598 us
  waiting for transfers between devices  216 us (36%)
  blocking collectives  206 us (34%)
  other arithmetic  96.6 us (16%)
  matrix products  55.3 us (9%)
  between operations  14.2 us (2%)
  local copies, waits for them, and re-layouts  10.3 us (2%)
    reduce_scatter x4, waiting for transfers between devices, local(): share = lax.psum_scatter(proj_part, 'prec', scatter_dimension=0, tiled=True)  161 us
    all_gather x4, blocking collectives, local(): gram_v = jnp.sum(lax.all_gather(gram_part, 'prec'), axis=0)  93.7 us
    all_gather x4, blocking collectives, local(): u_now = lax.all_gather(fresh, 'prec', axis=0, tiled=True)  79.3 us
    psum x4, waiting for transfers between devices, local(): lax.psum(proj_part.astype(jnp.bfloat16), 'run').astype(jnp.float32)  54.4 us
    another operation x24, other arithmetic, ridge_solve(): jnp.linalg.cholesky(gram + ridge_value * jnp.eye(size, dtype=jnp.float32))  52.3 us
    another operation x16, other arithmetic, ridge_solve(): return jax.scipy.linalg.cho_solve((factor, True), matrix.T).T  43.9 us
    psum x4, blocking collectives, local(): lax.psum(gram_part.astype(jnp.bfloat16), 'run').astype(jnp.float32)  32.7 us
    dot_general x4, matrix products, local(): proj_part = jnp.dot(resid, v_now, preferred_element_type=jnp.float32)  17.3 us
  transfers between devices with their start and end apart: 8, of which 8 were waited for; matrix products, arithmetic and copies ran while one was open for 9% of the time, Pallas kernels for 0%

profile of v1, /device:TPU:0, one launch (start us, length us, event | category | flops | bytes accessed | tf_op | source)
XLA Modules:
  0.0 598.5 jit_solution(11315393526274863771)
XLA Ops:
  10.3 5.5 copy.32
  20.7 24.6 %all-gather = f32[1024,64]{1,0:T(8,128)S(1)} all-gather(f32[64,64]{1,0:T(8,128)S(1)} %fusion.103), channel_id=2, replica_groups=mesh['prec'=16,'run'=2] {'prec'}, dimensions={0}, use_global_device_ids=true | all-gather | bytes 278528 | tf_op jit(solution)/shard_map/all_gather | solution.py:41
  45.5 5.8 cholesky.134
  52.7 4.9 custom-call.18
  57.6 21.6 %reduce-scatter.5.cloned.1.call-done = f32[32,64]{1,0:T(8,128)} async-done(((f32[512,64]{1,0:T(8,128)}), f32[32,64]{1,0:T(8,128)}) %reduce-scatter.5.cloned.1.call-update) | async-done | bytes 8208 | tf_op jit(solution)/shard_map/reduce_scatter | solution.py:42
  80.5 19.8 %all_gather.38 = bf16[512,64]{1,0:T(8,128)(2,1)S(1)} all-gather(bf16[32,64]{1,0:T(8,128)(2,1)S(1)} %fusion.31), channel_id=1, replica_groups=mesh['prec'=16,'run'=2] {'prec'}, dimensions={0}, use_global_device_ids=true | all-gather | bytes 69632 | tf_op jit(solution)/shard_map/all_gather | solution.py:48
  104.8 8.1 %psum.56 = bf16[64,64]{0,1:T(8,128)(2,1)S(1)} all-reduce(bf16[64,64]{0,1:T(8,128)(2,1)S(1)} %convolution_convert_fusion.11), channel_id=1, replica_groups=mesh['prec'=16,'run'=2] {'run'}, use_global_device_ids=true, to_apply=%region_4.7 | all-reduce | flops 4096 | bytes 16384 | tf_op jit(solution)/shard_map/psum | solution.py:56
  113.0 5.8 cholesky.145
  120.2 4.9 custom-call.19
  125.1 13.6 %all-reduce.5.cloned.1.call-done = bf16[2048,64]{0,1:T(8,128)(2,1)} async-done(((bf16[2048,64]{0,1:T(8,128)(2,1)}), bf16[2048,64]{0,1:T(8,128)(2,1)}) %all-reduce.5.cloned.1.call-update) | async-done | bytes 262160 | tf_op jit(solution)/shard_map/psum | solution.py:55
  145.6 23.3 %all-gather.1 = f32[1024,64]{1,0:T(8,128)S(1)} all-gather(f32[64,64]{1,0:T(8,128)S(1)} %fusion.104), channel_id=3, replica_groups=mesh['prec'=16,'run'=2] {'prec'}, dimensions={0}, use_global_device_ids=true | all-gather | bytes 278528 | tf_op jit(solution)/shard_map/all_gather | solution.py:41
  169.2 5.9 cholesky.156
  181.3 46.6 %reduce-scatter.7.cloned.1.call-done = f32[32,64]{1,0:T(8,128)} async-done(((f32[512,64]{1,0:T(8,128)}), f32[32,64]{1,0:T(8,128)}) %reduce-scatter.7.cloned.1.call-update) | async-done | bytes 8208 | tf_op jit(solution)/shard_map/reduce_scatter | solution.py:42
  229.2 19.8 %all_gather.41 = bf16[512,64]{1,0:T(8,128)(2,1)S(1)} all-gather(bf16[32,64]{1,0:T(8,128)(2,1)S(1)} %fusion.32), channel_id=1, replica_groups=mesh['prec'=16,'run'=2] {'prec'}, dimensions={0}, use_global_device_ids=true | all-gather | bytes 69632 | tf_op jit(solution)/shard_map/all_gather | solution.py:48
  253.5 8.1 %psum.58 = bf16[64,64]{0,1:T(8,128)(2,1)S(1)} all-reduce(bf16[64,64]{0,1:T(8,128)(2,1)S(1)} %convolution_convert_fusion.10), channel_id=1, replica_groups=mesh['prec'=16,'run'=2] {'run'}, use_global_device_ids=true, to_apply=%region_8.0 | all-reduce | flops 4096 | bytes 16384 | tf_op jit(solution)/shard_map/psum | solution.py:56
  261.7 5.8 cholesky.167
  273.8 13.6 %all-reduce.7.cloned.1.call-done = bf16[2048,64]{0,1:T(8,128)(2,1)} async-done(((bf16[2048,64]{0,1:T(8,128)(2,1)}), bf16[2048,64]{0,1:T(8,128)(2,1)}) %all-reduce.7.cloned.1.call-update) | async-done | bytes 262160 | tf_op jit(solution)/shard_map/psum | solution.py:55
  294.3 22.9 %all-gather.2 = f32[1024,64]{1,0:T(8,128)S(1)} all-gather(f32[64,64]{1,0:T(8,128)S(1)} %fusion.105), channel_id=4, replica_groups=mesh['prec'=16,'run'=2] {'prec'}, dimensions={0}, use_global_device_ids=true | all-gather | bytes 278528 | tf_op jit(solution)/shard_map/all_gather | solution.py:41
  317.4 5.9 cholesky.178
  329.6 46.6 %reduce-scatter.9.cloned.1.call-done = f32[32,64]{1,0:T(8,128)} async-done(((f32[512,64]{1,0:T(8,128)}), f32[32,64]{1,0:T(8,128)}) %reduce-scatter.9.cloned.1.call-update) | async-done | bytes 8208 | tf_op jit(solution)/shard_map/reduce_scatter | solution.py:42
  377.4 19.9 %all_gather.44 = bf16[512,64]{1,0:T(8,128)(2,1)S(1)} all-gather(bf16[32,64]{1,0:T(8,128)(2,1)S(1)} %fusion.33), channel_id=1, replica_groups=mesh['prec'=16,'run'=2] {'prec'}, dimensions={0}, use_global_device_ids=true | all-gather | bytes 69632 | tf_op jit(solution)/shard_map/all_gather | solution.py:48
  401.9 8.1 %psum.60 = bf16[64,64]{0,1:T(8,128)(2,1)S(1)} all-reduce(bf16[64,64]{0,1:T(8,128)(2,1)S(1)} %convolution_convert_fusion.9), channel_id=1, replica_groups=mesh['prec'=16,'run'=2] {'run'}, use_global_device_ids=true, to_apply=%region_12.0 | all-reduce | flops 4096 | bytes 16384 | tf_op jit(solution)/shard_map/psum | solution.py:56
  410.1 5.8 cholesky.189
  422.2 13.6 %all-reduce.9.cloned.1.call-done = bf16[2048,64]{0,1:T(8,128)(2,1)} async-done(((bf16[2048,64]{0,1:T(8,128)(2,1)}), bf16[2048,64]{0,1:T(8,128)(2,1)}) %all-reduce.9.cloned.1.call-update) | async-done | bytes 262160 | tf_op jit(solution)/shard_map/psum | solution.py:55
  442.7 22.9 %all-gather.3 = f32[1024,64]{1,0:T(8,128)S(1)} all-gather(f32[64,64]{1,0:T(8,128)S(1)} %fusion.106), channel_id=5, replica_groups=mesh['prec'=16,'run'=2] {'prec'}, dimensions={0}, use_global_device_ids=true | all-gather | bytes 278528 | tf_op jit(solution)/shard_map/all_gather | solution.py:41
  465.8 5.9 cholesky.200
  478.0 46.6 %reduce-scatter.11.cloned.1.call-done = f32[32,64]{1,0:T(8,128)} async-done(((f32[512,64]{1,0:T(8,128)}), f32[32,64]{1,0:T(8,128)}) %reduce-scatter.11.cloned.1.call-update) | async-done | bytes 8208 | tf_op jit(solution)/shard_map/reduce_scatter | solution.py:42
  525.8 19.8 %all_gather.47 = bf16[512,64]{1,0:T(8,128)(2,1)S(1)} all-gather(bf16[32,64]{1,0:T(8,128)(2,1)S(1)} %fusion.34), channel_id=1, replica_groups=mesh['prec'=16,'run'=2] {'prec'}, dimensions={0}, use_global_device_ids=true | all-gather | bytes 69632 | tf_op jit(solution)/shard_map/all_gather | solution.py:48
  550.1 8.3 %psum.62 = bf16[64,64]{0,1:T(8,128)(2,1)S(1)} all-reduce(bf16[64,64]{0,1:T(8,128)(2,1)S(1)} %convolution_convert_fusion.8), channel_id=1, replica_groups=mesh['prec'=16,'run'=2] {'run'}, use_global_device_ids=true, to_apply=%region_16.20 | all-reduce | flops 4096 | bytes 16384 | tf_op jit(solution)/shard_map/psum | solution.py:56
  558.6 5.8 cholesky.211
  565.7 4.9 custom-call.25
  570.6 13.6 %all-reduce.11.cloned.1.call-done = bf16[2048,64]{0,1:T(8,128)(2,1)} async-done(((bf16[2048,64]{0,1:T(8,128)(2,1)}), bf16[2048,64]{0,1:T(8,128)(2,1)}) %all-reduce.11.cloned.1.call-update) | async-done | bytes 262160 | tf_op jit(solution)/shard_map/psum | solution.py:55
  (128 shorter events, 95.7 us)
Async XLA Ops:
  6.5 9.4 %copy-start = (bf16[2048,64]{0,1:T(8,128)(2,1)S(1)}, bf16[2048,64]{0,1:T(8,128)(2,1)}, u32[]{:S(2)}) copy-start(bf16[2048,64]{0,1:T(8,128)(2,1)} %param.12) | copy-start | bytes 786436
  6.5 72.6 %reduce-scatter.5.cloned.1.call-start = ((), (), s32[]{:S(2)}) async-start(), calls=%async_computation.4 | async-start | bytes 278528 | tf_op jit(solution)/shard_map/reduce_scatter | solution.py:42
  10.3 5.7 copy-start.1
  10.3 5.7 copy-start.2
  20.4 118.3 %all-reduce.5.cloned.1.call-start = ((), (), s32[]{:S(2)}) async-start(), calls=%async_computation.5 | async-start | bytes 524288 | tf_op jit(solution)/shard_map/psum | solution.py:55
  118.9 109.1 %reduce-scatter.7.cloned.1.call-start = ((), (), s32[]{:S(2)}) async-start(), calls=%async_computation.6 | async-start | bytes 278528 | tf_op jit(solution)/shard_map/reduce_scatter | solution.py:42
  175.8 111.6 %all-reduce.7.cloned.1.call-start = ((), (), s32[]{:S(2)}) async-start(), calls=%async_computation.7 | async-start | bytes 524288 | tf_op jit(solution)/shard_map/psum | solution.py:55
  267.6 108.6 %reduce-scatter.9.cloned.1.call-start = ((), (), s32[]{:S(2)}) async-start(), calls=%async_computation.8 | async-start | bytes 278528 | tf_op jit(solution)/shard_map/reduce_scatter | solution.py:42
  324.0 111.8 %all-reduce.9.cloned.1.call-start = ((), (), s32[]{:S(2)}) async-start(), calls=%async_computation.9 | async-start | bytes 524288 | tf_op jit(solution)/shard_map/psum | solution.py:55
  416.0 108.6 %reduce-scatter.11.cloned.1.call-start = ((), (), s32[]{:S(2)}) async-start(), calls=%async_computation.10 | async-start | bytes 278528 | tf_op jit(solution)/shard_map/reduce_scatter | solution.py:42
  472.4 111.8 %all-reduce.11.cloned.1.call-start = ((), (), s32[]{:S(2)}) async-start(), calls=%async_computation.11 | async-start | bytes 524288 | tf_op jit(solution)/shard_map/psum | solution.py:55
Sparse Core Ops, SparseCore 0:
  20.5 58.5 reduce-scatter.4
  119.0 19.6 all-reduce.4
  175.9 52.0 reduce-scatter.6
  267.8 19.5 all-reduce.6
  324.1 52.0 reduce-scatter.8
  416.2 19.5 all-reduce.8
  472.5 52.0 reduce-scatter.10
  564.6 19.5 all-reduce.10
